TPU v7x, 32 devices: a whole 2x2x4 slice. The times are simulated.
32 devices in a mesh: scene: 2 (over x), along: 16 (over z, y, core).
Axes of the slice: x: 2, y: 2, z: 4, core: 2. Of those that a mesh axis runs over, the one named last changes fastest.
Arguments:
- echoes: bfloat16 [2, 64, 16, 16, 256], P(None, ('scene', 'along')), parts along dimension 1, may hold values from -6 to 6
- integer_cell_displacement: int32 [64, 16], P(('scene', 'along')), parts along dimension 0, may hold values from 0 to 15
- fractional_level_label: int32 [64, 16], P(('scene', 'along')), parts along dimension 0, may hold values from 0 to 15
- steering: bfloat16 [2, 256, 256], replicated, may hold values from -0.25 to 0.25
- tile_anchor: int32 [32], P('scene'), parts along dimension 0, may hold values from -64 to 3904, as said below
Outputs:
- image_tiles: bfloat16 [2, 8192, 256], P(None, ('scene', 'along')), parts along dimension 1
There are 2 independent parts, one for each index of `scene`. A program takes and returns all parts, laid end to end along the dimension named above; an argument that names none is the same for every part. Nothing has to cross between parts.
Inputs may be any that keep to these rules, and one draw needn't show every extreme that they name: tile_anchor[j] lies within 64 of j * 256.
All inputs are finite; a program needn't handle non-finite values.
Results may differ from a plain program's by a relative error of at most 0.0064.
Values may be sent and summed in bfloat16 or wider, within the bound.
A program may use at most 64 MiB of HBM per device.

v0:
```python
import functools
import math

import jax
import jax.numpy as jnp
import numpy as np
from jax import lax
from jax.experimental import pallas as pl
from jax.experimental.pallas import tpu as pltpu
from jax.sharding import PartitionSpec as P

TILE_X = 256
STEPS = 16
TAPS = 8
SHIFTS = 16
FRACTION_LEVELS = 16
QUAD = 4093
WAVE_FOURTHS = 37
GROUP = 4
REACH = STEPS // GROUP
HALVES = 2
MESH = pl.DeviceIdType.MESH


def half_turn_fit(function, powers):
    spots = 0.5005 * np.cos(np.pi * (np.arange(400) + 0.5) / 800)
    table = np.stack([spots ** (2 * power) for power in range(powers)], 1)
    return [float(c) for c in np.linalg.lstsq(table, function(spots), rcond=None)[0]]


SIN_FIT = half_turn_fit(lambda f: np.sin(np.pi * f) / f, 5)
COS_FIT = half_turn_fit(lambda f: np.cos(np.pi * f), 6)


def horner(coefficients, square):
    value = coefficients[-1]
    for coefficient in coefficients[-2::-1]:
        value = value * square + coefficient
    return value


def tap_weights(integer_cell_displacement, fractional_level_label):
    fraction = fractional_level_label.astype(jnp.float32) / FRACTION_LEVELS
    tap_place = jnp.arange(TAPS, dtype=jnp.float32) - (TAPS // 2 - 1)
    displacement = tap_place[None, None, :] - fraction[..., None]
    window_taper = 0.54 + 0.46 * jnp.cos(math.pi * displacement / (TAPS // 2))
    kernel = jnp.sinc(displacement) * window_taper
    angle_turns = jnp.mod(
        WAVE_FOURTHS * (integer_cell_displacement * FRACTION_LEVELS + fractional_level_label),
        4 * FRACTION_LEVELS,
    ).astype(jnp.float32) / (4 * FRACTION_LEVELS)
    phase_angle = 2.0 * math.pi * angle_turns
    return (kernel * jnp.cos(phase_angle)[..., None], -kernel * jnp.sin(phase_angle)[..., None])


def beams_kernel(cells, weight_real, weight_imag, echoes, steering, beams, straight, crossed):
    _, pulses, transmitters, receivers, bins = echoes.shape
    part = bins // HALVES
    lanes = lax.broadcasted_iota(jnp.int32, (2 * receivers, bins), 1)
    reach_back = SHIFTS // 2 + TAPS // 2 - 1
    for pulse in range(pulses):

        @pl.loop(0, transmitters)
        def _(sender):
            cell = cells[pulse, sender] - reach_back
            both = jnp.concatenate([echoes[0, pulse, sender], echoes[1, pulse, sender]], 0)
            both = pltpu.roll(both.astype(jnp.float32), lax.rem(bins - cell, bins), 1)
            place = lanes + cell
            real = imag = None
            for tap in range(TAPS):
                moved = both if tap == 0 else pltpu.roll(both, bins - tap, 1)
                inside = (place >= -tap) & (place < bins - tap)
                moved = jnp.where(inside, moved, 0.0)
                a, b = moved[:receivers], moved[receivers:]
                wr = weight_real[pulse, sender * TAPS + tap]
                wi = weight_imag[pulse, sender * TAPS + tap]
                add_real = wr * a - wi * b
                add_imag = wr * b + wi * a
                real = add_real if real is None else real + add_real
                imag = add_imag if imag is None else imag + add_imag
            rows = pl.ds(pl.multiple_of(sender * receivers, receivers), receivers)
            minus = (-imag).astype(jnp.bfloat16)
            real, imag = real.astype(jnp.bfloat16), imag.astype(jnp.bfloat16)
            for half in range(HALVES):
                cut = slice(half * part, (half + 1) * part)
                straight[pulse, half, rows, :part] = real[:, cut]
                straight[pulse, half, rows, part:] = imag[:, cut]
                crossed[pulse, half, rows, :part] = minus[:, cut]
                crossed[pulse, half, rows, part:] = real[:, cut]

        contract = functools.partial(
            lax.dot_general,
            dimension_numbers=(((0,), (0,)), ((), ())),
            preferred_element_type=jnp.float32,
        )
        for half in range(HALVES):
            formed = contract(steering[0], straight[pulse, half])
            formed = formed + contract(steering[1], crossed[pulse, half])
            beams[half, pulse] = formed.astype(jnp.bfloat16)


def image_kernel(
    count, anchors, own, image, got, crossed, table, total, outgoing, incoming,
    mate_send, mate_recv, side_send, side_recv, pass_send, pass_recv, up_send, up_recv,
):
    _, pulses, beams, width = own.shape
    part = width // 2
    spacing = TILE_X // pulses
    blocks = GROUP * pulses + 1
    me = lax.axis_index("along")
    group, place = me // GROUP, me % GROUP
    groups = count // GROUP
    mate = group * GROUP + (place + 1 - 2 * (place % 2))
    side = group * GROUP + (place + 2) % GROUP
    mate_place, side_place = mate % GROUP, side % GROUP
    far_place = side_place + 1 - 2 * (side_place % 2)
    has_below, has_above = group > 0, group < groups - 1

    barrier = pltpu.get_barrier_semaphore()
    for other in (mate, side):
        pl.semaphore_signal(barrier, inc=1, device_id={"along": other}, device_id_type=MESH)

    @pl.when(has_below)
    def _():
        pl.semaphore_signal(barrier, inc=1, device_id={"along": me - GROUP}, device_id_type=MESH)

    @pl.when(has_above)
    def _():
        pl.semaphore_signal(barrier, inc=1, device_id={"along": me + GROUP}, device_id_type=MESH)

    pl.semaphore_wait(barrier, 2 + has_below.astype(jnp.int32) + has_above.astype(jnp.int32))

    def remote(source, landing, send, recv, device):
        return pltpu.make_async_remote_copy(
            src_ref=source, dst_ref=landing, send_sem=send, recv_sem=recv,
            device_id={"along": device}, device_id_type=MESH,
        )

    def to_side(half):
        return remote(own.at[half], got.at[place, half], side_send.at[half], side_recv.at[half], side)

    def to_mate(half):
        return remote(own.at[half], got.at[place, half], mate_send.at[half], mate_recv.at[half], mate)

    def pass_on(half):
        return remote(
            got.at[side_place, half], got.at[side_place, half],
            pass_send.at[half], pass_recv.at[half], mate,
        )

    def to_above(step, half):
        return remote(
            outgoing.at[step - 1, half], incoming.at[step - 1, half],
            up_send.at[step - 1, half], up_recv.at[step - 1, half], me + GROUP,
        )

    for half in range(HALVES):
        to_side(half).start()
    for half in range(HALVES):
        to_mate(half).start()

    def reaches(step):
        return group + step < groups

    gain = (STEPS * pulses * beams) ** (-0.5)
    beam = lax.broadcasted_iota(jnp.int32, (8, beams), 1)
    beam = beam.astype(jnp.float32)
    beam_square = beam * beam
    beam_square = beam_square - QUAD * jnp.floor(beam_square * (1.0 / QUAD) + 0.5)
    row = lax.broadcasted_iota(jnp.int32, (16, beams), 0)
    beam = jnp.concatenate([beam, beam], 0)
    beam_square = jnp.concatenate([beam_square, beam_square], 0)

    def wrap(value):
        return value - QUAD * jnp.floor(value * (1.0 / QUAD) + 0.5)

    for step in range(REACH, -1, -1):

        @pl.when(reaches(step))
        def _(step=step):
            tile = (group + step) * GROUP + place
            first = anchors[tile] - TILE_X * (group * GROUP + GROUP - 1) - spacing * (pulses - 1)

            @pl.loop(0, blocks * spacing // 16, unroll=4)
            def _(slab):
                offset = wrap((first + slab * 16 + row).astype(jnp.float32))
                square = wrap(offset * offset)
                units = wrap(square + beam_square * offset + beam * square)
                turn = units * (1.0 / QUAD)
                fine = turn * turn
                sine = turn * horner(SIN_FIT, fine)
                cosine = horner(COS_FIT, fine)
                rows = pl.ds(pl.multiple_of(slab * 16, 16), 16)
                table[step, rows, :beams] = (gain - (2 * gain) * (sine * sine)).astype(jnp.bfloat16)
                table[step, rows, beams:] = ((2 * gain) * sine * cosine).astype(jnp.bfloat16)

    def project(step, half):
        total[step, half] = jnp.zeros((TILE_X, width), jnp.float32)
        low = place + 1 if step == REACH else 0
        high = place + 1 if step == 0 else GROUP

        @pl.loop(low, high)
        def _(source):
            value = None
            for pulse in range(pulses):
                start = (GROUP - 1 - source) * TILE_X + spacing * (pulses - 1 - pulse)
                rows = pl.ds(pl.multiple_of(start, 128), TILE_X)
                term = jnp.dot(
                    table[step, rows, :beams], got[source, half, pulse],
                    preferred_element_type=jnp.float32,
                ) + jnp.dot(
                    table[step, rows, beams:], crossed[source, half, pulse],
                    preferred_element_type=jnp.float32,
                )
                value = term if value is None else value + term
            total[step, half] += value

    def send_up(step, half):
        outgoing[step - 1, half] = total[step, half].astype(jnp.bfloat16)
        to_above(step, half).start()

    def finish(half):
        cut = slice(half * part, (half + 1) * part)
        image[0, :, cut] = total[0, half, :, :part].astype(jnp.bfloat16)
        image[1, :, cut] = total[0, half, :, part:].astype(jnp.bfloat16)

    for half in range(HALVES):
        got[place, half] = own[half]
        to_side(half).wait_recv()
        pass_on(half).start()
        to_mate(half).wait_recv()
        pass_on(half).wait_recv()
        for source in range(GROUP):
            for pulse in range(pulses):
                crossed[source, half, pulse, :, :part] = -got[source, half, pulse, :, part:]
                crossed[source, half, pulse, :, part:] = got[source, half, pulse, :, :part]
        for step in range(REACH, -1, -1):

            @pl.when(reaches(step))
            def _(step=step, half=half):
                project(step, half)
                if step == REACH:
                    send_up(step, half)
                elif step > 0:
                    pl.when(jnp.logical_not(has_below))(lambda: send_up(step, half))

    for half in range(HALVES):
        for step in range(REACH - 1, -1, -1):

            @pl.when(has_below & reaches(step))
            def _(step=step, half=half):
                to_above(step + 1, half).wait_recv()
                total[step, half] += incoming[step, half].astype(jnp.float32)
                if step > 0:
                    send_up(step, half)

        finish(half)

    for half in range(HALVES):
        to_side(half).wait_send()
        to_mate(half).wait_send()
        pass_on(half).wait_send()
        for step in range(1, REACH + 1):
            pl.when(reaches(step))(lambda step=step, half=half: to_above(step, half).wait_send())


def local(count, echoes, integer_cell_displacement, fractional_level_label, steering, tile_anchor):
    _, pulses, transmitters, receivers, bins = echoes.shape
    channels, beams = steering.shape[1:]
    part = bins // HALVES
    width = 2 * part
    weight_real, weight_imag = tap_weights(integer_cell_displacement, fractional_level_label)
    smem = pl.BlockSpec(memory_space=pltpu.SMEM)
    vmem = pl.BlockSpec(memory_space=pltpu.VMEM)
    beam_data = pl.pallas_call(
        beams_kernel,
        out_shape=jax.ShapeDtypeStruct((HALVES, pulses, beams, width), jnp.bfloat16),
        in_specs=[smem, smem, smem, vmem, vmem],
        out_specs=vmem,
        scratch_shapes=[
            pltpu.VMEM((pulses, HALVES, channels, width), jnp.bfloat16),
            pltpu.VMEM((pulses, HALVES, channels, width), jnp.bfloat16),
        ],
        name="beams",
    )(
        integer_cell_displacement,
        weight_real.reshape(pulses, transmitters * TAPS),
        weight_imag.reshape(pulses, transmitters * TAPS),
        echoes,
        steering,
    )
    rows = (GROUP * pulses + 1) * (TILE_X // pulses)
    pair = (HALVES,)
    dma = pltpu.SemaphoreType.DMA
    return pl.pallas_call(
        functools.partial(image_kernel, count),
        out_shape=jax.ShapeDtypeStruct((2, TILE_X, bins), jnp.bfloat16),
        in_specs=[smem, vmem],
        out_specs=vmem,
        scratch_shapes=[
            pltpu.VMEM((GROUP, HALVES, pulses, beams, width), jnp.bfloat16),
            pltpu.VMEM((GROUP, HALVES, pulses, beams, width), jnp.bfloat16),
            pltpu.VMEM((REACH + 1, rows, 2 * beams), jnp.bfloat16),
            pltpu.VMEM((REACH + 1, HALVES, TILE_X, width), jnp.float32),
            pltpu.VMEM((REACH, HALVES, TILE_X, width), jnp.bfloat16),
            pltpu.VMEM((REACH, HALVES, TILE_X, width), jnp.bfloat16),
            dma(pair), dma(pair), dma(pair), dma(pair), dma(pair), dma(pair),
            dma((REACH, HALVES)), dma((REACH, HALVES)),
        ],
        compiler_params=pltpu.CompilerParams(
            collective_id=0, has_side_effects=True, vmem_limit_bytes=48 * 1024 * 1024
        ),
        name="image",
    )(tile_anchor, beam_data)


def solution(mesh):
    placed = (
        P(None, ("scene", "along"), None, None, None),
        P(("scene", "along"), None),
        P(("scene", "along"), None),
        P(),
        P("scene"),
    )
    return jax.shard_map(
        functools.partial(local, mesh.shape["along"]),
        mesh=mesh,
        in_specs=placed,
        out_specs=P(None, ("scene", "along"), None),
        check_vma=False,
    )
```

profile of v0, /device:TPU:30, one launch (start us, length us, event | category | flops | bytes accessed | tf_op | source)
XLA Modules:
  0.0 48.5 jit_solution(1906088922720148083)
XLA Ops:
  0.0 0.0 copy-start.2
  0.0 0.7 %copy-done.2 = s32[2,16]{1,0:T(2,128)S(1)} copy-done((s32[2,16]{1,0:T(2,128)S(1)}, s32[2,16]{1,0:T(2,128)}, u32[]{:S(2)}) %copy-start.2) | copy-done | bytes 152
  0.7 0.8 %fusion.8 = (f32[2,16]{1,0:T(2,128)S(1)}, f32[2,16]{1,0:T(2,128)S(1)}, f32[2,16]{1,0:T(2,128)S(1)}) fusion(s32[2,16]{1,0:T(2,128)} %param.7, s32[2,16]{1,0:T(2,128)S(1)} %copy-done.2), kind=kLoop, calls=%fused_computation.23 | loop fusion | flops 576 | bytes 640 | tf_op jit(solution)/shard_map/sin | solution.py:53
  1.5 0.1 sub.38
  1.6 0.1 mul.151
  1.7 0.1 mul.152
  1.8 0.1 mul.154
  1.9 0.1 mul.155
  2.0 0.1 sub.40
  2.0 0.1 sub.41
  2.1 0.6 %negate_multiply_fusion = (f32[2,128]{1,0:T(2,128)}, f32[2,128]{1,0:T(2,128)S(1)}) fusion(f32[2,128]{1,0:T(2,128)S(1)} %mul.155, f32[2,128]{1,0:T(2,128)S(1)} %sub.41, f32[128]{0:T(128)S(1)} %sub.38), kind=kLoop, calls=%fused_computation.11 | loop fusion | flops 10240 | bytes 4608 | tf_op jit(solution)/shard_map/mul | solution.py:53
  2.7 0.6 %mul.153.weight_real = f32[2,128]{1,0:T(2,128)} multiply(f32[2,128]{1,0:T(2,128)S(1)} %get-tuple-element.6, f32[2,128]{1,0:T(2,128)S(1)} %mul.152) | non-fusion elementwise | flops 256 | bytes 3072 | tf_op jit(solution)/shard_map/mul | solution.py:53
  3.3 0.0 copy-start.1
  3.3 9.2 %beams.1.own = bf16[2,2,256,256]{3,2,1,0:T(8,128)(2,1)} custom-call(s32[2,16]{1,0:T(2,128)} %cells.1, f32[2,128]{1,0:T(2,128)} %mul.153.weight_real, f32[2,128]{1,0:T(2,128)} %get-tuple-element.5.weight_imag, bf16[2,2,16,16,256]{4,3,2,1,0:T(8,128)(2,1)} %echoes.1, bf16[2,256,256]{2,1,0:T(8,128)(2,1)} %steering.1), custom_call_target="tpu_custom_call" | custom-call | tf_op jit(solution)/shard_map/beams/pallas_call | solution.py:275
  12.5 0.0 copy-done.1
  12.5 0.0 copy-start
  12.5 1.0 %copy-done = bf16[2,2,256,256]{3,2,1,0:T(8,128)(2,1)S(1)} copy-done((bf16[2,2,256,256]{3,2,1,0:T(8,128)(2,1)S(1)}, bf16[2,2,256,256]{3,2,1,0:T(8,128)(2,1)}, u32[]{:S(2)}) %copy-start) | copy-done | bytes 524312
  13.6 34.2 %image.1 = bf16[2,256,256]{2,1,0:T(8,128)(2,1)S(1)} custom-call(s32[16]{0:T(128)S(1)} %copy-done.1, bf16[2,2,256,256]{3,2,1,0:T(8,128)(2,1)S(1)} %copy-done), custom_call_target="tpu_custom_call" | custom-call | tf_op jit(solution)/shard_map/image/pallas_call | solution.py:295
  47.8 0.7 %copy.7 = bf16[2,256,256]{2,1,0:T(8,128)(2,1)} copy(bf16[2,256,256]{2,1,0:T(8,128)(2,1)S(1)} %image.1) | data formatting | bytes 524288
  (3 shorter events, 0.1 us)
Async XLA Ops:
  0.0 0.7 %copy-start.2 = (s32[2,16]{1,0:T(2,128)S(1)}, s32[2,16]{1,0:T(2,128)}, u32[]{:S(2)}) copy-start(s32[2,16]{1,0:T(2,128)} %cells.1) | copy-start | bytes 388
  3.3 9.2 %copy-start.1 = (s32[16]{0:T(128)S(1)}, s32[16]{0:T(128)}, u32[]{:S(2)}) copy-start(s32[16]{0:T(128)} %anchors.1) | copy-start | bytes 196
  12.5 1.0 %copy-start = (bf16[2,2,256,256]{3,2,1,0:T(8,128)(2,1)S(1)}, bf16[2,2,256,256]{3,2,1,0:T(8,128)(2,1)}, u32[]{:S(2)}) copy-start(bf16[2,2,256,256]{3,2,1,0:T(8,128)(2,1)} %beams.1.own) | copy-start | bytes 1572868
where the time goes:
time: 48.9 us; the launch traced here: 48.5 us
  Pallas kernels  43.4 us (89%)
  local copies, waits for them, and re-layouts  3.03 us (6%)
  other arithmetic  2.01 us (4%)
    pallas_call x1, Pallas kernels, local(): pl.pallas_call(functools.partial(image_kernel, count), out_shape=jax.Shap...  34.2 us
    pallas_call x1, Pallas kernels, local(): pl.pallas_call(beams_kernel, out_shape=jax.ShapeDtypeStruct((HALVES, puls...  9.21 us
    unnamed x7, local copies, waits for them, and re-layouts  2.42 us

commit v1 on v0

v1 whole, which is shorter than its diff:
```python
import functools
import math

import jax
import jax.numpy as jnp
import numpy as np
from jax import lax
from jax.experimental import pallas as pl
from jax.experimental.pallas import tpu as pltpu
from jax.sharding import PartitionSpec as P

TILE_X = 256
STEPS = 16
TAPS = 8
SHIFTS = 16
FRACTION_LEVELS = 16
QUAD = 4093
WAVE_FOURTHS = 37
GROUP = 4
REACH = STEPS // GROUP
HALVES = 2
MESH = pl.DeviceIdType.MESH


def half_turn_fit(function, powers):
    spots = 0.5005 * np.cos(np.pi * (np.arange(400) + 0.5) / 800)
    table = np.stack([spots ** (2 * power) for power in range(powers)], 1)
    return [float(c) for c in np.linalg.lstsq(table, function(spots), rcond=None)[0]]


SIN_FIT = half_turn_fit(lambda f: np.sin(np.pi * f) / f, 5)
COS_FIT = half_turn_fit(lambda f: np.cos(np.pi * f), 6)


def horner(coefficients, square):
    value = coefficients[-1]
    for coefficient in coefficients[-2::-1]:
        value = value * square + coefficient
    return value


def wrap(value):
    return value - QUAD * jnp.floor(value * (1.0 / QUAD) + 0.5)


def tap_weights(cell, level):
    shape = (TAPS, 128)
    tap = lax.broadcasted_iota(jnp.int32, shape, 0)
    fraction = jnp.full(shape, level, jnp.int32).astype(jnp.float32) * (1.0 / FRACTION_LEVELS)
    displacement = (tap - (TAPS // 2 - 1)).astype(jnp.float32) - fraction
    short = jnp.minimum(fraction, 1.0 - fraction)
    sine = short * horner(SIN_FIT, short * short)
    sine = jnp.where(tap % 2 == (TAPS // 2) % 2, sine, -sine)
    centre = displacement == 0.0
    kernel = jnp.where(centre, 1.0, sine / (math.pi * jnp.where(centre, 1.0, displacement)))
    quarter = displacement * (1.0 / TAPS)
    quarter_sine = quarter * horner(SIN_FIT, quarter * quarter)
    kernel = kernel * (0.54 + 0.46 * (1.0 - 2.0 * (quarter_sine * quarter_sine)))
    cycle = 4 * FRACTION_LEVELS
    units = lax.rem(WAVE_FOURTHS * (cell * FRACTION_LEVELS + level), cycle)
    turn = jnp.full(shape, units, jnp.int32).astype(jnp.float32) * (1.0 / cycle)
    turn = jnp.where(turn > 0.5, turn - 1.0, turn)
    half_sine = turn * horner(SIN_FIT, turn * turn)
    half_cosine = horner(COS_FIT, turn * turn)
    real = kernel * (1.0 - 2.0 * (half_sine * half_sine))
    imag = kernel * (-2.0 * (half_sine * half_cosine))
    return real, imag


def compensate(pulse, cells, levels, echoes, straight, crossed_rows):
    _, _, transmitters, receivers, bins = echoes.shape
    part = bins // HALVES
    lanes = lax.broadcasted_iota(jnp.int32, (2 * receivers, bins), 1)
    reach_back = SHIFTS // 2 + TAPS // 2 - 1

    @pl.loop(0, transmitters, unroll=4)
    def _(sender):
        own_cell = cells[pulse, sender]
        cell = own_cell - reach_back
        weight_real, weight_imag = tap_weights(own_cell, levels[pulse, sender])
        weight_real = jnp.concatenate([weight_real] * (bins // 128), 1)
        weight_imag = jnp.concatenate([weight_imag] * (bins // 128), 1)
        both = jnp.concatenate([echoes[0, pulse, sender], echoes[1, pulse, sender]], 0)
        both = pltpu.roll(both.astype(jnp.float32), lax.rem(bins - cell, bins), 1)
        place = lanes + cell
        real = imag = None
        for tap in range(TAPS):
            moved = both if tap == 0 else pltpu.roll(both, bins - tap, 1)
            inside = (place >= -tap) & (place < bins - tap)
            moved = jnp.where(inside, moved, 0.0)
            a, b = moved[:receivers], moved[receivers:]
            wr = weight_real[tap : tap + 1]
            wi = weight_imag[tap : tap + 1]
            add_real = wr * a - wi * b
            add_imag = wr * b + wi * a
            real = add_real if real is None else real + add_real
            imag = add_imag if imag is None else imag + add_imag
        rows = pl.ds(pl.multiple_of(sender * receivers, receivers), receivers)
        minus = (-imag).astype(jnp.bfloat16)
        real, imag = real.astype(jnp.bfloat16), imag.astype(jnp.bfloat16)
        for half in range(HALVES):
            cut = slice(half * part, (half + 1) * part)
            straight[half, rows, :part] = real[:, cut]
            straight[half, rows, part:] = imag[:, cut]
            crossed_rows[half, rows, :part] = minus[:, cut]
            crossed_rows[half, rows, part:] = real[:, cut]


def image_kernel(
    count, anchors, cells, levels, echoes, steering, image,
    straight, crossed_rows, turned, got, crossed, table, total, outgoing, incoming,
    mate_send, mate_recv, side_send, side_recv, pass_send, pass_recv, up_send, up_recv,
):
    pulses = echoes.shape[1]
    beams = steering.shape[2]
    part = echoes.shape[4] // HALVES
    width = 2 * part
    spacing = TILE_X // pulses
    blocks = GROUP * pulses + 1
    me = lax.axis_index("along")
    group, place = me // GROUP, me % GROUP
    groups = count // GROUP
    mate = group * GROUP + (place + 1 - 2 * (place % 2))
    side = group * GROUP + (place + 2) % GROUP
    mate_place, side_place = mate % GROUP, side % GROUP
    far_place = side_place + 1 - 2 * (side_place % 2)
    has_below, has_above = group > 0, group < groups - 1

    barrier = pltpu.get_barrier_semaphore()
    for other in (mate, side):
        pl.semaphore_signal(barrier, inc=1, device_id={"along": other}, device_id_type=MESH)

    @pl.when(has_below)
    def _():
        pl.semaphore_signal(barrier, inc=1, device_id={"along": me - GROUP}, device_id_type=MESH)

    @pl.when(has_above)
    def _():
        pl.semaphore_signal(barrier, inc=1, device_id={"along": me + GROUP}, device_id_type=MESH)


    def remote(source, landing, send, recv, device):
        return pltpu.make_async_remote_copy(
            src_ref=source, dst_ref=landing, send_sem=send, recv_sem=recv,
            device_id={"along": device}, device_id_type=MESH,
        )

    def to_side(half, pulse):
        mine = got.at[place, half, pulse]
        return remote(mine, mine, side_send.at[half, pulse], side_recv.at[half, pulse], side)

    def to_mate(half, pulse):
        mine = got.at[place, half, pulse]
        return remote(mine, mine, mate_send.at[half, pulse], mate_recv.at[half, pulse], mate)

    def pass_on(half, pulse):
        theirs = got.at[side_place, half, pulse]
        return remote(theirs, theirs, pass_send.at[half, pulse], pass_recv.at[half, pulse], mate)

    def to_above(step, half):
        return remote(
            outgoing.at[step - 1, half], incoming.at[step - 1, half],
            up_send.at[step - 1, half], up_recv.at[step - 1, half], me + GROUP,
        )

    turned[0] = steering[0].T
    turned[1] = steering[1].T

    def form(pulse, half):
        formed = jnp.dot(turned[0], straight[half], preferred_element_type=jnp.float32)
        formed += jnp.dot(turned[1], crossed_rows[half], preferred_element_type=jnp.float32)
        got[place, half, pulse] = formed.astype(jnp.bfloat16)

    for pulse in range(pulses):
        compensate(pulse, cells, levels, echoes, straight, crossed_rows)
        form(pulse, 0)
        if pulse == 0:
            pl.semaphore_wait(
                barrier, 2 + has_below.astype(jnp.int32) + has_above.astype(jnp.int32)
            )
        to_side(0, pulse).start()
        to_mate(0, pulse).start()
        for half in range(1, HALVES):
            form(pulse, half)
    for half in range(1, HALVES):
        for pulse in range(pulses):
            to_side(half, pulse).start()
            to_mate(half, pulse).start()

    def reaches(step):
        return group + step < groups

    gain = (STEPS * pulses * beams) ** (-0.5)
    beam = lax.broadcasted_iota(jnp.int32, (8, beams), 1)
    beam = beam.astype(jnp.float32)
    beam_square = beam * beam
    beam_square = beam_square - QUAD * jnp.floor(beam_square * (1.0 / QUAD) + 0.5)
    row = lax.broadcasted_iota(jnp.int32, (16, beams), 0)
    beam = jnp.concatenate([beam, beam], 0)
    beam_square = jnp.concatenate([beam_square, beam_square], 0)

    def make_table(step):

        @pl.when(reaches(step))
        def _():
            tile = (group + step) * GROUP + place
            first = anchors[tile] - TILE_X * (group * GROUP + GROUP - 1) - spacing * (pulses - 1)

            @pl.loop(0, blocks * spacing // 16, unroll=4)
            def _(slab):
                offset = wrap((first + slab * 16 + row).astype(jnp.float32))
                square = wrap(offset * offset)
                units = wrap(square + beam_square * offset + beam * square)
                turn = units * (1.0 / QUAD)
                fine = turn * turn
                sine = turn * horner(SIN_FIT, fine)
                cosine = horner(COS_FIT, fine)
                rows = pl.ds(pl.multiple_of(slab * 16, 16), 16)
                table[step, rows, :beams] = (gain - (2 * gain) * (sine * sine)).astype(jnp.bfloat16)
                table[step, rows, beams:] = ((2 * gain) * sine * cosine).astype(jnp.bfloat16)

    for step in range(REACH, 1, -1):
        make_table(step)

    def project(step, half):
        total[step, half] = jnp.zeros((TILE_X, width), jnp.float32)
        low = place + 1 if step == REACH else 0
        high = place + 1 if step == 0 else GROUP

        @pl.loop(low, high)
        def _(source):
            value = None
            for pulse in range(pulses):
                start = (GROUP - 1 - source) * TILE_X + spacing * (pulses - 1 - pulse)
                rows = pl.ds(pl.multiple_of(start, 128), TILE_X)
                term = jnp.dot(
                    table[step, rows, :beams], got[source, half, pulse],
                    preferred_element_type=jnp.float32,
                ) + jnp.dot(
                    table[step, rows, beams:], crossed[source, half, pulse],
                    preferred_element_type=jnp.float32,
                )
                value = term if value is None else value + term
            total[step, half] += value

    def send_up(step, half):
        outgoing[step - 1, half] = total[step, half].astype(jnp.bfloat16)
        to_above(step, half).start()

    def finish(half):
        cut = slice(half * part, (half + 1) * part)
        image[0, :, cut] = total[0, half, :, :part].astype(jnp.bfloat16)
        image[1, :, cut] = total[0, half, :, part:].astype(jnp.bfloat16)

    for half in range(HALVES):
        for pulse in range(pulses):
            to_side(half, pulse).wait_recv()
            pass_on(half, pulse).start()
        for pulse in range(pulses):
            to_mate(half, pulse).wait_recv()
            pass_on(half, pulse).wait_recv()
        for source in range(GROUP):
            for pulse in range(pulses):
                crossed[source, half, pulse, :, :part] = -got[source, half, pulse, :, part:]
                crossed[source, half, pulse, :, part:] = got[source, half, pulse, :, :part]
        for step in range(REACH, -1, -1):
            if half == 0 and step <= 1:
                make_table(step)

            @pl.when(reaches(step))
            def _(step=step, half=half):
                project(step, half)
                if step == REACH:
                    send_up(step, half)
                elif step > 0:
                    pl.when(jnp.logical_not(has_below))(lambda: send_up(step, half))

    for half in range(HALVES):
        for step in range(REACH - 1, -1, -1):

            @pl.when(has_below & reaches(step))
            def _(step=step, half=half):
                to_above(step + 1, half).wait_recv()
                total[step, half] += incoming[step, half].astype(jnp.float32)
                if step > 0:
                    send_up(step, half)

        finish(half)

    for half in range(HALVES):
        for pulse in range(pulses):
            to_side(half, pulse).wait_send()
            to_mate(half, pulse).wait_send()
            pass_on(half, pulse).wait_send()
        for step in range(1, REACH + 1):
            pl.when(reaches(step))(lambda step=step, half=half: to_above(step, half).wait_send())


def local(count, echoes, integer_cell_displacement, fractional_level_label, steering, tile_anchor):
    pulses, bins = echoes.shape[1], echoes.shape[4]
    channels, beams = steering.shape[1:]
    part = bins // HALVES
    width = 2 * part
    smem = pl.BlockSpec(memory_space=pltpu.SMEM)
    vmem = pl.BlockSpec(memory_space=pltpu.VMEM)
    rows = (GROUP * pulses + 1) * (TILE_X // pulses)
    pair = (HALVES, pulses)
    dma = pltpu.SemaphoreType.DMA
    return pl.pallas_call(
        functools.partial(image_kernel, count),
        out_shape=jax.ShapeDtypeStruct((2, TILE_X, bins), jnp.bfloat16),
        in_specs=[smem, smem, smem, vmem, vmem],
        out_specs=vmem,
        scratch_shapes=[
            pltpu.VMEM((HALVES, channels, width), jnp.bfloat16),
            pltpu.VMEM((HALVES, channels, width), jnp.bfloat16),
            pltpu.VMEM((2, beams, channels), jnp.bfloat16),
            pltpu.VMEM((GROUP, HALVES, pulses, beams, width), jnp.bfloat16),
            pltpu.VMEM((GROUP, HALVES, pulses, beams, width), jnp.bfloat16),
            pltpu.VMEM((REACH + 1, rows, 2 * beams), jnp.bfloat16),
            pltpu.VMEM((REACH + 1, HALVES, TILE_X, width), jnp.float32),
            pltpu.VMEM((REACH, HALVES, TILE_X, width), jnp.bfloat16),
            pltpu.VMEM((REACH, HALVES, TILE_X, width), jnp.bfloat16),
            dma(pair), dma(pair), dma(pair), dma(pair), dma(pair), dma(pair),
            dma((REACH, HALVES)), dma((REACH, HALVES)),
        ],
        compiler_params=pltpu.CompilerParams(
            collective_id=0, has_side_effects=True, vmem_limit_bytes=48 * 1024 * 1024
        ),
        name="image",
    )(tile_anchor, integer_cell_displacement, fractional_level_label, echoes, steering)


def solution(mesh):
    placed = (
        P(None, ("scene", "along"), None, None, None),
        P(("scene", "along"), None),
        P(("scene", "along"), None),
        P(),
        P("scene"),
    )
    return jax.shard_map(
        functools.partial(local, mesh.shape["along"]),
        mesh=mesh,
        in_specs=placed,
        out_specs=P(None, ("scene", "along"), None),
        check_vma=False,
    )
```

time: 48.9 us -> 42.9 us (0.88)
  Pallas kernels: 43.4 us -> 38 us
  other arithmetic: 2.01 us -> 0 us
  local copies, waits for them, and re-layouts: 3.03 us -> 4.71 us
    pallas_call x1 -> x0, Pallas kernels: 9.21 us -> none  [local(): pl.pallas_call(beams_kernel, out_shape=jax.ShapeDtypeStruct((HALVES, puls...]
    pallas_call x1, Pallas kernels: 34.2 us -> 38 us  [local(): pl.pallas_call(functools.partial(image_kernel, count), out_shape=jax.Shap...]
    unnamed x7 -> x11, local copies, waits for them, and re-layouts: 2.42 us -> 4.71 us
    mul x2 -> x0, other arithmetic: 1.2 us -> none  [the longest x1 0.62 us: tap_weights(): -kernel * jnp.sin(phase_angle)[..., None]]
    sin x1 -> x0, other arithmetic: 0.8 us -> none  [tap_weights(): jnp.sin(phase_angle)[..., None]]
where the time goes in v1:
time: 42.9 us; the launch traced here: 42.7 us
  Pallas kernels  38 us (89%)
  local copies, waits for them, and re-layouts  4.71 us (11%)
    pallas_call x1, Pallas kernels, local(): pl.pallas_call(functools.partial(image_kernel, count), out_shape=jax.Shap...  38 us
    unnamed x11, local copies, waits for them, and re-layouts  4.71 us

profile of v1, /device:TPU:30, one launch (start us, length us, event | category | flops | bytes accessed | tf_op | source)
XLA Modules:
  0.0 42.7 jit_solution(12190950994376098248)
XLA Ops:
  0.0 0.0 copy-start
  0.0 1.0 %copy-done = bf16[2,2,16,16,256]{4,3,2,1,0:T(8,128)(2,1)S(1)} copy-done((bf16[2,2,16,16,256]{4,3,2,1,0:T(8,128)(2,1)S(1)}, bf16[2,2,16,16,256]{4,3,2,1,0:T(8,128)(2,1)}, u32[]{:S(2)}) %copy-start) | copy-done | bytes 524312
  1.0 0.0 copy-start.1
  1.0 0.9 %copy-done.1 = bf16[2,256,256]{2,1,0:T(8,128)(2,1)S(1)} copy-done((bf16[2,256,256]{2,1,0:T(8,128)(2,1)S(1)}, bf16[2,256,256]{2,1,0:T(8,128)(2,1)}, u32[]{:S(2)}) %copy-start.1) | copy-done | bytes 262168
  2.0 0.0 copy-start.2
  2.0 0.7 %copy-done.2 = s32[2,16]{1,0:T(2,128)S(1)} copy-done((s32[2,16]{1,0:T(2,128)S(1)}, s32[2,16]{1,0:T(2,128)}, u32[]{:S(2)}) %copy-start.2) | copy-done | bytes 152
  2.7 0.0 copy-start.3
  2.7 0.7 %copy-done.3 = s32[2,16]{1,0:T(2,128)S(1)} copy-done((s32[2,16]{1,0:T(2,128)S(1)}, s32[2,16]{1,0:T(2,128)}, u32[]{:S(2)}) %copy-start.3) | copy-done | bytes 152
  3.4 0.0 copy-start.4
  3.4 0.7 %copy-done.4 = s32[16]{0:T(128)S(1)} copy-done((s32[16]{0:T(128)S(1)}, s32[16]{0:T(128)}, u32[]{:S(2)}) %copy-start.4) | copy-done | bytes 88
  4.0 38.0 %image.1 = bf16[2,256,256]{2,1,0:T(8,128)(2,1)S(1)} custom-call(s32[16]{0:T(128)S(1)} %copy-done.4, s32[2,16]{1,0:T(2,128)S(1)} %copy-done.2, s32[2,16]{1,0:T(2,128)S(1)} %copy-done.3, bf16[2,2,16,16,256]{4,3,2,1,0:T(8,128)(2,1)S(1)} %copy-done, bf16[2,256,256]{2,1,0:T(8,128)(2,1)S(1)} %copy-done.1), custom_call_target="tpu_custom_call" | custom-call | tf_op jit(solution)/shard_map/image/pallas_call | solution.py:309
  42.0 0.7 %copy.7 = bf16[2,256,256]{2,1,0:T(8,128)(2,1)} copy(bf16[2,256,256]{2,1,0:T(8,128)(2,1)S(1)} %image.1) | data formatting | bytes 524288
Async XLA Ops:
  0.0 1.0 %copy-start = (bf16[2,2,16,16,256]{4,3,2,1,0:T(8,128)(2,1)S(1)}, bf16[2,2,16,16,256]{4,3,2,1,0:T(8,128)(2,1)}, u32[]{:S(2)}) copy-start(bf16[2,2,16,16,256]{4,3,2,1,0:T(8,128)(2,1)} %echoes.1) | copy-start | bytes 1572868
  1.0 0.9 %copy-start.1 = (bf16[2,256,256]{2,1,0:T(8,128)(2,1)S(1)}, bf16[2,256,256]{2,1,0:T(8,128)(2,1)}, u32[]{:S(2)}) copy-start(bf16[2,256,256]{2,1,0:T(8,128)(2,1)} %steering.1) | copy-start | bytes 786436
  2.0 0.7 %copy-start.2 = (s32[2,16]{1,0:T(2,128)S(1)}, s32[2,16]{1,0:T(2,128)}, u32[]{:S(2)}) copy-start(s32[2,16]{1,0:T(2,128)} %cells.1) | copy-start | bytes 388
  2.7 0.7 %copy-start.3 = (s32[2,16]{1,0:T(2,128)S(1)}, s32[2,16]{1,0:T(2,128)}, u32[]{:S(2)}) copy-start(s32[2,16]{1,0:T(2,128)} %levels.1) | copy-start | bytes 388
  3.4 0.7 %copy-start.4 = (s32[16]{0:T(128)S(1)}, s32[16]{0:T(128)}, u32[]{:S(2)}) copy-start(s32[16]{0:T(128)} %anchors.1) | copy-start | bytes 196

commit v2 on v1

--- a/solution.py
+++ b/solution.py
@@ -107,7 +107,8 @@
 
 
 def image_kernel(
-    count, anchors, cells, levels, echoes, steering, image,
+    count, far_anchors, far_cells, far_levels, far_echoes, far_steering, image,
+    anchors, cells, levels, echoes, steering, fetched,
     straight, crossed_rows, turned, got, crossed, table, total, outgoing, incoming,
     mate_send, mate_recv, side_send, side_recv, pass_send, pass_recv, up_send, up_recv,
 ):
@@ -117,6 +118,16 @@
     width = 2 * part
     spacing = TILE_X // pulses
     blocks = GROUP * pulses + 1
+    fetches = [
+        pltpu.make_async_copy(source, landing, fetched.at[number])
+        for number, (source, landing) in enumerate(
+            [(far_cells, cells), (far_levels, levels), (far_steering, steering), (far_anchors, anchors)]
+            + [(far_echoes.at[:, pulse], echoes.at[:, pulse]) for pulse in range(pulses)]
+        )
+    ]
+    fetch_cells, fetch_levels, fetch_steering, fetch_anchors, *fetch_echoes = fetches
+    for fetch in (fetch_cells, fetch_levels, *fetch_echoes, fetch_steering, fetch_anchors):
+        fetch.start()
     me = lax.axis_index("along")
     group, place = me // GROUP, me % GROUP
     groups = count // GROUP
@@ -163,16 +174,21 @@
             up_send.at[step - 1, half], up_recv.at[step - 1, half], me + GROUP,
         )
 
-    turned[0] = steering[0].T
-    turned[1] = steering[1].T
-
     def form(pulse, half):
         formed = jnp.dot(turned[0], straight[half], preferred_element_type=jnp.float32)
         formed += jnp.dot(turned[1], crossed_rows[half], preferred_element_type=jnp.float32)
         got[place, half, pulse] = formed.astype(jnp.bfloat16)
 
     for pulse in range(pulses):
+        if pulse == 0:
+            fetch_cells.wait()
+            fetch_levels.wait()
+        fetch_echoes[pulse].wait()
         compensate(pulse, cells, levels, echoes, straight, crossed_rows)
+        if pulse == 0:
+            fetch_steering.wait()
+            turned[0] = steering[0].T
+            turned[1] = steering[1].T
         form(pulse, 0)
         if pulse == 0:
             pl.semaphore_wait(
@@ -219,6 +235,7 @@
                 table[step, rows, :beams] = (gain - (2 * gain) * (sine * sine)).astype(jnp.bfloat16)
                 table[step, rows, beams:] = ((2 * gain) * sine * cosine).astype(jnp.bfloat16)
 
+    fetch_anchors.wait()
     for step in range(REACH, 1, -1):
         make_table(step)
 
@@ -252,7 +269,7 @@
         image[0, :, cut] = total[0, half, :, :part].astype(jnp.bfloat16)
         image[1, :, cut] = total[0, half, :, part:].astype(jnp.bfloat16)
 
-    for half in range(HALVES):
+    def collect(half):
         for pulse in range(pulses):
             to_side(half, pulse).wait_recv()
             pass_on(half, pulse).start()
@@ -263,29 +280,44 @@
             for pulse in range(pulses):
                 crossed[source, half, pulse, :, :part] = -got[source, half, pulse, :, part:]
                 crossed[source, half, pulse, :, part:] = got[source, half, pulse, :, :part]
-        for step in range(REACH, -1, -1):
-            if half == 0 and step <= 1:
-                make_table(step)
-
-            @pl.when(reaches(step))
-            def _(step=step, half=half):
-                project(step, half)
-                if step == REACH:
-                    send_up(step, half)
-                elif step > 0:
-                    pl.when(jnp.logical_not(has_below))(lambda: send_up(step, half))
-
-    for half in range(HALVES):
-        for step in range(REACH - 1, -1, -1):
-
-            @pl.when(has_below & reaches(step))
-            def _(step=step, half=half):
-                to_above(step + 1, half).wait_recv()
-                total[step, half] += incoming[step, half].astype(jnp.float32)
-                if step > 0:
-                    send_up(step, half)
-
-        finish(half)
+
+    def begin(step, half):
+
+        @pl.when(reaches(step))
+        def _():
+            project(step, half)
+            if step == REACH:
+                send_up(step, half)
+            elif step > 0:
+                pl.when(jnp.logical_not(has_below))(lambda: send_up(step, half))
+
+    def combine(step, half):
+
+        @pl.when(has_below & reaches(step))
+        def _():
+            to_above(step + 1, half).wait_recv()
+            total[step, half] += incoming[step, half].astype(jnp.float32)
+            if step > 0:
+                send_up(step, half)
+
+    collect(0)
+    for step in range(REACH, -1, -1):
+        if step <= 1:
+            make_table(step)
+        begin(step, 0)
+    for step in range(REACH - 1, 1, -1):
+        combine(step, 0)
+    collect(1)
+    for step in range(REACH, 1, -1):
+        begin(step, 1)
+    combine(1, 0)
+    for step in range(1, -1, -1):
+        begin(step, 1)
+    combine(0, 0)
+    finish(0)
+    for step in range(REACH - 1, -1, -1):
+        combine(step, 1)
+    finish(1)
 
     for half in range(HALVES):
         for pulse in range(pulses):
@@ -301,17 +333,21 @@
     channels, beams = steering.shape[1:]
     part = bins // HALVES
     width = 2 * part
-    smem = pl.BlockSpec(memory_space=pltpu.SMEM)
-    vmem = pl.BlockSpec(memory_space=pltpu.VMEM)
     rows = (GROUP * pulses + 1) * (TILE_X // pulses)
     pair = (HALVES, pulses)
     dma = pltpu.SemaphoreType.DMA
     return pl.pallas_call(
         functools.partial(image_kernel, count),
         out_shape=jax.ShapeDtypeStruct((2, TILE_X, bins), jnp.bfloat16),
-        in_specs=[smem, smem, smem, vmem, vmem],
-        out_specs=vmem,
+        in_specs=[pl.BlockSpec(memory_space=pltpu.HBM)] * 5,
+        out_specs=pl.BlockSpec(memory_space=pltpu.VMEM),
         scratch_shapes=[
+            pltpu.SMEM(tile_anchor.shape, jnp.int32),
+            pltpu.SMEM(integer_cell_displacement.shape, jnp.int32),
+            pltpu.SMEM(fractional_level_label.shape, jnp.int32),
+            pltpu.VMEM(echoes.shape, echoes.dtype),
+            pltpu.VMEM(steering.shape, steering.dtype),
+            dma((4 + pulses,)),
             pltpu.VMEM((HALVES, channels, width), jnp.bfloat16),
             pltpu.VMEM((HALVES, channels, width), jnp.bfloat16),
             pltpu.VMEM((2, beams, channels), jnp.bfloat16),
@@ -325,7 +361,7 @@
             dma((REACH, HALVES)), dma((REACH, HALVES)),
         ],
         compiler_params=pltpu.CompilerParams(
-            collective_id=0, has_side_effects=True, vmem_limit_bytes=48 * 1024 * 1024
+            collective_id=0, has_side_effects=True, vmem_limit_bytes=67_043_328
         ),
         name="image",
     )(tile_anchor, integer_cell_displacement, fractional_level_label, echoes, steering)

time: 42.9 us -> 38.3 us (0.89)
  local copies, waits for them, and re-layouts: 4.71 us -> 1.67 us
  Pallas kernels: 38 us -> 36.1 us
    unnamed x11 -> x1, local copies, waits for them, and re-layouts: 4.71 us -> 1.67 us
    pallas_call x1, Pallas kernels: 38 us -> 36.1 us  [local(): pl.pallas_call(functools.partial(image_kernel, count), out_shape=jax.Shap...]
where the time goes in v2:
time: 38.3 us; the launch traced here: 37.8 us
  Pallas kernels  36.1 us (94%)
  local copies, waits for them, and re-layouts  1.67 us (4%)
    pallas_call x1, Pallas kernels, local(): pl.pallas_call(functools.partial(image_kernel, count), out_shape=jax.Shap...  36.1 us
    unnamed x1, local copies, waits for them, and re-layouts  1.67 us

profile of v2, /device:TPU:30, one launch (start us, length us, event | category | flops | bytes accessed | tf_op | source)
XLA Modules:
  0.0 37.8 jit_solution(6049272669373813672)
XLA Ops:
  0.0 36.1 %image.1 = bf16[2,256,256]{2,1,0:T(8,128)(2,1)} custom-call(s32[16]{0:T(128)} %far_anchors.1, s32[2,16]{1,0:T(2,128)} %far_cells.1, s32[2,16]{1,0:T(2,128)} %far_levels.1, bf16[2,2,16,16,256]{4,3,2,1,0:T(8,128)(2,1)} %far_echoes.1, bf16[2,256,256]{2,1,0:T(8,128)(2,1)} %far_steering.1), custom_call_target="tpu_custom_call" | custom-call | tf_op jit(solution)/shard_map/image/pallas_call | solution.py:339
  36.1 1.7 %copy.7 = bf16[2,256,256]{2,1,0:T(8,128)(2,1)} copy(bf16[2,256,256]{2,1,0:T(8,128)(2,1)} %image.1) | data formatting | bytes 524288

commit v3 on v2

--- a/solution.py
+++ b/solution.py
@@ -19,6 +19,7 @@
 GROUP = 4
 REACH = STEPS // GROUP
 HALVES = 2
+STRIPS = 2
 MESH = pl.DeviceIdType.MESH
 
 
@@ -168,10 +169,13 @@
         theirs = got.at[side_place, half, pulse]
         return remote(theirs, theirs, pass_send.at[half, pulse], pass_recv.at[half, pulse], mate)
 
-    def to_above(step, half):
+    strip = TILE_X // STRIPS
+
+    def to_above(step, half, number):
+        rows = pl.ds(number * strip, strip)
         return remote(
-            outgoing.at[step - 1, half], incoming.at[step - 1, half],
-            up_send.at[step - 1, half], up_recv.at[step - 1, half], me + GROUP,
+            outgoing.at[step - 1, half, rows], incoming.at[step - 1, half, rows],
+            up_send.at[step - 1, half, number], up_recv.at[step - 1, half, number], me + GROUP,
         )
 
     def form(pulse, half):
@@ -236,8 +240,6 @@
                 table[step, rows, beams:] = ((2 * gain) * sine * cosine).astype(jnp.bfloat16)
 
     fetch_anchors.wait()
-    for step in range(REACH, 1, -1):
-        make_table(step)
 
     def project(step, half):
         total[step, half] = jnp.zeros((TILE_X, width), jnp.float32)
@@ -260,19 +262,25 @@
                 value = term if value is None else value + term
             total[step, half] += value
 
+    def send_strip(step, half, number):
+        rows = pl.ds(number * strip, strip)
+        outgoing[step - 1, half, rows] = total[step, half, rows].astype(jnp.bfloat16)
+        to_above(step, half, number).start()
+
     def send_up(step, half):
-        outgoing[step - 1, half] = total[step, half].astype(jnp.bfloat16)
-        to_above(step, half).start()
+        for number in range(STRIPS):
+            send_strip(step, half, number)
 
     def finish(half):
         cut = slice(half * part, (half + 1) * part)
         image[0, :, cut] = total[0, half, :, :part].astype(jnp.bfloat16)
         image[1, :, cut] = total[0, half, :, part:].astype(jnp.bfloat16)
 
+    def forward(half, pulse):
+        to_side(half, pulse).wait_recv()
+        pass_on(half, pulse).start()
+
     def collect(half):
-        for pulse in range(pulses):
-            to_side(half, pulse).wait_recv()
-            pass_on(half, pulse).start()
         for pulse in range(pulses):
             to_mate(half, pulse).wait_recv()
             pass_on(half, pulse).wait_recv()
@@ -295,29 +303,38 @@
 
         @pl.when(has_below & reaches(step))
         def _():
-            to_above(step + 1, half).wait_recv()
-            total[step, half] += incoming[step, half].astype(jnp.float32)
-            if step > 0:
-                send_up(step, half)
-
-    collect(0)
-    for step in range(REACH, -1, -1):
-        if step <= 1:
-            make_table(step)
-        begin(step, 0)
-    for step in range(REACH - 1, 1, -1):
-        combine(step, 0)
-    collect(1)
-    for step in range(REACH, 1, -1):
-        begin(step, 1)
-    combine(1, 0)
-    for step in range(1, -1, -1):
-        begin(step, 1)
-    combine(0, 0)
-    finish(0)
-    for step in range(REACH - 1, -1, -1):
-        combine(step, 1)
-    finish(1)
+            for number in range(STRIPS):
+                rows = pl.ds(number * strip, strip)
+                to_above(step + 1, half, number).wait_recv()
+                total[step, half, rows] += incoming[step, half, rows].astype(jnp.float32)
+                if step > 0:
+                    send_strip(step, half, number)
+
+    for step in range(REACH, 2, -1):
+        make_table(step)
+    forward(0, 0)
+    make_table(2)
+    for pulse in range(1, pulses):
+        forward(0, pulse)
+    for half in range(HALVES):
+        if half > 0:
+            for pulse in range(pulses):
+                forward(half, pulse)
+        collect(half)
+        for step in range(REACH, 1, -1):
+            begin(step, half)
+        if half > 0:
+            combine(1, half - 1)
+        for step in range(1, -1, -1):
+            if half == 0:
+                make_table(step)
+            begin(step, half)
+        for step in range(REACH - 1, 1, -1):
+            combine(step, half)
+    combine(1, HALVES - 1)
+    for half in range(HALVES):
+        combine(0, half)
+        finish(half)
 
     for half in range(HALVES):
         for pulse in range(pulses):
@@ -325,7 +342,8 @@
             to_mate(half, pulse).wait_send()
             pass_on(half, pulse).wait_send()
         for step in range(1, REACH + 1):
-            pl.when(reaches(step))(lambda step=step, half=half: to_above(step, half).wait_send())
+            for number in range(STRIPS):
+                pl.when(reaches(step))(to_above(step, half, number).wait_send)
 
 
 def local(count, echoes, integer_cell_displacement, fractional_level_label, steering, tile_anchor):
@@ -358,7 +376,7 @@
             pltpu.VMEM((REACH, HALVES, TILE_X, width), jnp.bfloat16),
             pltpu.VMEM((REACH, HALVES, TILE_X, width), jnp.bfloat16),
             dma(pair), dma(pair), dma(pair), dma(pair), dma(pair), dma(pair),
-            dma((REACH, HALVES)), dma((REACH, HALVES)),
+            dma((REACH, HALVES, STRIPS)), dma((REACH, HALVES, STRIPS)),
         ],
         compiler_params=pltpu.CompilerParams(
             collective_id=0, has_side_effects=True, vmem_limit_bytes=67_043_328

time: 38.3 us -> 36.8 us (0.961)
  Pallas kernels: 36.1 us -> 34.5 us
    pallas_call x1, Pallas kernels: 36.1 us -> 34.5 us  [local(): pl.pallas_call(functools.partial(image_kernel, count), out_shape=jax.Shap...]
where the time goes in v3:
time: 36.8 us; the launch traced here: 36.2 us
  Pallas kernels  34.5 us (94%)
  local copies, waits for them, and re-layouts  1.67 us (5%)
    pallas_call x1, Pallas kernels, local(): pl.pallas_call(functools.partial(image_kernel, count), out_shape=jax.Shap...  34.5 us
    unnamed x1, local copies, waits for them, and re-layouts  1.67 us

profile of v3, /device:TPU:30, one launch (start us, length us, event | category | flops | bytes accessed | tf_op | source)
XLA Modules:
  0.0 36.2 jit_solution(16329334295282842689)
XLA Ops:
  0.0 34.5 %image.1 = bf16[2,256,256]{2,1,0:T(8,128)(2,1)} custom-call(s32[16]{0:T(128)} %far_anchors.1, s32[2,16]{1,0:T(2,128)} %far_cells.1, s32[2,16]{1,0:T(2,128)} %far_levels.1, bf16[2,2,16,16,256]{4,3,2,1,0:T(8,128)(2,1)} %far_echoes.1, bf16[2,256,256]{2,1,0:T(8,128)(2,1)} %far_steering.1), custom_call_target="tpu_custom_call" | custom-call | tf_op jit(solution)/shard_map/image/pallas_call | solution.py:357
  34.6 1.7 %copy.7 = bf16[2,256,256]{2,1,0:T(8,128)(2,1)} copy(bf16[2,256,256]{2,1,0:T(8,128)(2,1)} %image.1) | data formatting | bytes 524288
